TPU v7x, 32 devices: a whole 2x2x4 slice. The times are simulated.
32 devices in a mesh: row: 2 (over y), col: 16 (over z, x, core).
Axes of the slice: x: 2, y: 2, z: 4, core: 2. Of those that a mesh axis runs over, the one named last changes fastest.
Arguments:
- blocks: bfloat16 [128, 2048, 128], P('row', 'col'), may hold values from -0.1875 to 0.1875
- block_rows: int32 [2, 1024], P('row', 'col'), may hold values from 0 to 2047, as said below
- block_cols: int32 [2, 1024], P('row', 'col'), may hold values from 0 to 255
- counts: int32 [2, 16], P('row', 'col'), may hold values from 1 to 64, as said below
- start_vectors: float32 [32, 524288], P(None, ('row', 'col')), may hold values from -6 to 6
Outputs:
- vectors: float32 [32, 524288], P(None, ('row', 'col'))
Inputs may be any that keep to these rules, and one draw needn't show every extreme that they name: counts[r, c] is the number of live slots of grid position (r, c); in every draw some position has all 64 slots live. For every grid position (r, c) and every o < 16, exactly 4 of its 64 slots have block_rows[r, c * 64 + s] // 128 == o.
All inputs are finite; a program needn't handle non-finite values.
Results may differ from a plain program's by a relative error of at most 0.0036.
Values may be sent and summed in bfloat16 or wider, within the bound.
A program may use at most 256 MiB of HBM per device.

v0:
```python
import math
import jax
import jax.numpy as jnp
from jax import lax
from jax.sharding import PartitionSpec as P

N = 524288
ITERS = 2


def cholesky_lower(gram_matrix):
    matrix_order = gram_matrix.shape[0]
    positions = jnp.arange(matrix_order)

    def column_step(position, factor):
        before = (positions < position).astype(gram_matrix.dtype)
        target_row = lax.dynamic_index_in_dim(factor, position, 0, keepdims=False) * before
        column = lax.dynamic_index_in_dim(gram_matrix, position, 1, keepdims=False)
        residue = column - jnp.sum(factor * target_row[None, :], axis=1)
        on_diagonal = positions == position
        pivot_value = jnp.sqrt(jnp.sum(jnp.where(on_diagonal, residue, 0.0)))
        values = jnp.where(on_diagonal, pivot_value, residue / pivot_value)
        values = jnp.where(positions >= position, values, 0.0)
        return lax.dynamic_update_index_in_dim(factor, values, position, 1)

    return lax.fori_loop(0, matrix_order, column_step, jnp.zeros_like(gram_matrix))


def lower_inverse(lower_factor):
    matrix_order = lower_factor.shape[0]
    positions = jnp.arange(matrix_order)

    def row_step(position, inverse):
        lower_row = lax.dynamic_index_in_dim(lower_factor, position, 0, keepdims=False)
        before = (positions < position).astype(lower_factor.dtype)
        inner_sum = jnp.sum((lower_row * before)[:, None] * inverse, axis=0)
        unit_row = (positions == position).astype(lower_factor.dtype)
        pivot_value = jnp.sum(lower_row * unit_row)
        return lax.dynamic_update_index_in_dim(
            inverse, (unit_row - inner_sum) / pivot_value, position, 0
        )

    return lax.fori_loop(0, matrix_order, row_step, jnp.zeros_like(lower_factor))


def accumulate(blocks, rows_index, cols_index, live_count, row_panel, col_panel):
    slot_count, block_size = (blocks.shape[0], blocks.shape[1])
    vector_count = row_panel.shape[0]
    row_blocks = row_panel.reshape(vector_count, -1, block_size)
    col_blocks = col_panel.reshape(vector_count, -1, block_size)
    group_size = math.gcd(slot_count, 64)
    turn_count = (live_count + group_size - 1) // group_size
    slot_offsets = jnp.arange(group_size, dtype=jnp.int32)

    def one_group(turn_index, partial_sums):
        row_sums, col_sums = partial_sums
        first_slot = turn_index * group_size
        live_mask = (first_slot + slot_offsets < live_count).astype(jnp.float32)
        from_cols = jnp.take(col_blocks, cols_index, axis=1)
        from_rows = jnp.take(row_blocks, rows_index, axis=1)
        to_cols = jnp.einsum("kgi,gij->kgj", from_rows, blocks, preferred_element_type=jnp.float32)
        col_sums = col_sums.at[:, cols_index].add(to_cols * live_mask[None, :, None])
        to_rows = jnp.einsum("kgj,gij->kgi", from_cols, blocks, preferred_element_type=jnp.float32)
        row_sums = row_sums.at[:, rows_index].add(to_rows * live_mask[None, :, None])
        return (row_sums, col_sums)

    row_start = jnp.zeros(row_blocks.shape, jnp.float32)
    initial = (row_start, jnp.zeros(col_blocks.shape, jnp.float32))
    return lax.fori_loop(0, turn_count, one_group, initial)


def per_device(blocks, block_rows, block_cols, counts, start_vectors):
    live_count = counts[0, 0]
    rows_index = block_rows[0]
    cols_index = block_cols[0]
    vectors = start_vectors
    for iteration in range(ITERS):
        rounded = vectors.astype(jnp.bfloat16)
        vector_count = rounded.shape[0]
        col_panel = lax.all_gather(rounded, "row", axis=1, tiled=True)
        row_panel = lax.all_gather(rounded, "col", axis=1, tiled=True)
        row_sums, col_sums = accumulate(
            blocks, rows_index, cols_index, live_count, row_panel, col_panel
        )
        from_row_group = lax.psum_scatter(
            row_sums.reshape(vector_count, -1), "col", scatter_dimension=1, tiled=True
        )
        from_col_group = lax.psum_scatter(
            col_sums.reshape(vector_count, -1), "row", scatter_dimension=1, tiled=True
        )
        product = from_row_group + from_col_group
        local_gram = jnp.dot(
            product, product.T, precision=lax.Precision.HIGHEST, preferred_element_type=jnp.float32
        )
        gram_matrix = lax.psum(local_gram, ("row", "col")) / N
        inverse = lower_inverse(cholesky_lower(gram_matrix))
        vectors = jnp.dot(
            inverse, product, precision=lax.Precision.HIGHEST, preferred_element_type=jnp.float32
        )
    return vectors


def solution(mesh):
    placed = (
        P("row", "col", None),
        P("row", "col"),
        P("row", "col"),
        P("row", "col"),
        P(None, ("row", "col")),
    )
    return jax.shard_map(
        per_device, mesh=mesh, in_specs=placed, out_specs=P(None, ("row", "col")), check_vma=False
    )
```

profile of v0, /device:TPU:0, one launch (start us, length us, event | category | flops | bytes accessed | tf_op | source)
XLA Modules:
  0.0 1549.7 jit_solution(5209276909103308987)
XLA Ops:
  6.5 2.8 convert_element_type.66
  9.4 0.7 all-gather.7.cloned.1.call-update
  11.0 34.4 %all-gather.5.cloned.1.call-done = bf16[32,32768]{1,0:T(8,128)(2,1)} async-done(((bf16[32,16384]{1,0:T(8,128)(2,1)}), bf16[32,32768]{1,0:T(8,128)(2,1)}) %all-gather.5.cloned.1.call-update) | async-done | bytes 2097168 | tf_op jit(solution)/shard_map/all_gather | solution.py:80
  45.4 3.3 copy_bitcast_fusion.7
  48.6 2.2 gather_fusion
  50.9 2.2 fusion.34
  53.1 121.4 %all-gather.7.cloned.1.call-done = bf16[32,262144]{1,0:T(8,128)(2,1)} async-done(((bf16[32,16384]{1,0:T(8,128)(2,1)}), bf16[32,262144]{1,0:T(8,128)(2,1)}) %all-gather.7.cloned.1.call-update) | async-done | bytes 16777232 | tf_op jit(solution)/shard_map/all_gather | solution.py:81
  174.5 14.5 copy_bitcast_fusion.3
  189.0 6.4 gather_fusion.1
  195.4 1.7 fusion.32
  197.1 11.3 broadcast.314.clone
  208.4 2.6 broadcast.315.clone
  210.9 20.4 %while.90 = (s32[]{:T(128)}, f32[32,2048,128]{2,0,1:T(8,128)}, f32[32,256,128]{2,0,1:T(8,128)}, s32[]{:T(128)}, s32[64]{0:T(128)S(1)}, /*index=5*/s32[]{:T(128)}...) while((s32[]{:T(128)}, f32[32,2048,128]{2,0,1:T(8,128)}, ...), condition=%wide.region_3.6_spmd.clone, body=%wide.region_0.5_spmd.clone.sunk | while | flops 1049155 | bytes 10487937 | solution.py:69
  211.6 2.7 broadcast_multiply_fusion.8
  214.3 9.0 scatter_fusion
  223.3 8.0 scatter_fusion.1
  231.3 4.4 copy_bitcast_fusion.5
  235.8 22.6 %copy_bitcast_fusion.1 = f32[32,262144]{1,0:T(8,128)} fusion(f32[32,2048,128]{2,0,1:T(8,128)} %get-tuple-element.609), kind=kLoop, calls=%fused_computation.69 | loop fusion | bytes 67108864 | tf_op jit(solution)/shard_map/reshape | solution.py:86
  258.5 30.0 %reduce-scatter.7.cloned.1.call-done = f32[32,16384]{1,0:T(8,128)} async-done(((f32[32,32768]{1,0:T(8,128)}), f32[32,16384]{1,0:T(8,128)}) %reduce-scatter.7.cloned.1.call-update) | async-done | bytes 2097168 | tf_op jit(solution)/shard_map/reduce_scatter | solution.py:88
  288.4 337.4 %reduce-scatter.5.cloned.1.call-done = f32[32,16384]{1,0:T(8,128)} async-done(((f32[32,262144]{1,0:T(8,128)}), f32[32,16384]{1,0:T(8,128)}) %reduce-scatter.5.cloned.1.call-update) | async-done | bytes 2097168 | tf_op jit(solution)/shard_map/reduce_scatter | solution.py:85
  625.8 2.4 add.220
  628.2 1.3 copy-done.2
  629.5 1.8 fusion.52
  631.3 39.1 %psum.14 = f32[32,32]{1,0:T(8,128)S(1)} all-reduce(f32[32,32]{1,0:T(8,128)S(1)} %fusion.52), channel_id=1, replica_groups=mesh['row'=2,'col'=16] {'row','col'}, use_global_device_ids=true, to_apply=%region_6.9 | all-reduce | flops 1024 | bytes 8192 | tf_op jit(solution)/shard_map/psum | solution.py:95
  670.4 58.1 %while.92 = (s32[]{:T(128)}, f32[32,32]{1,0:T(8,128)S(1)}, f32[32,32]{0,1:T(8,128)S(1)}, s32[]{:T(128)}, s32[]{:T(128)}) while((s32[]{:T(128)}, f32[32,32]{1,0:T(8,128)S(1)}, f32[32,32]{0,1:T(8,128)S(1)}, s32[]{:T(128)}, s32[]{:T(128)}) %tuple.192), condition=%wide.region_10.13_spmd.clone.clone, body=%wide.region_7.12_spmd.clone.clone.sunk | while | flops 2401 | bytes 8913 | solution.py:26
  670.6 0.7 fusion.88
  672.3 0.7 fusion.88
  674.1 0.7 fusion.88
  676.0 0.7 fusion.88
  677.8 0.7 fusion.88
  679.6 0.7 fusion.88
  685.1 0.7 fusion.88
  690.5 0.7 fusion.88
  708.7 0.7 fusion.88
  714.2 0.7 fusion.88
  719.6 0.7 fusion.88
  725.1 0.7 fusion.88
  728.6 49.0 %while.93 = (s32[]{:T(128)}, f32[32,32]{1,0:T(8,128)S(1)}, f32[32,32]{1,0:T(8,128)S(1)}, s32[]{:T(128)}, s32[]{:T(128)}) while((s32[]{:T(128)}, f32[32,32]{1,0:T(8,128)S(1)}, f32[32,32]{1,0:T(8,128)S(1)}, s32[]{:T(128)}, s32[]{:T(128)}) %tuple.195), condition=%wide.region_14.17_spmd.clone.clone, body=%wide.region_11.16_spmd.clone.clone.sunk | while | flops 2305 | bytes 6221 | solution.py:43
  777.6 4.4 convolution_convert_fusion
  782.8 32.2 %all-gather.9.cloned.1.call-done = bf16[32,32768]{1,0:T(8,128)(2,1)} async-done(((bf16[32,16384]{1,0:T(8,128)(2,1)}), bf16[32,32768]{1,0:T(8,128)(2,1)}) %all-gather.9.cloned.1.call-update) | async-done | bytes 2097168 | tf_op jit(solution)/shard_map/all_gather | solution.py:80
  815.1 3.3 copy_bitcast_fusion.6
  818.3 2.2 gather_fusion.2
  820.6 2.2 fusion.30
  822.8 121.5 %all-gather.11.cloned.1.call-done = bf16[32,262144]{1,0:T(8,128)(2,1)} async-done(((bf16[32,16384]{1,0:T(8,128)(2,1)}), bf16[32,262144]{1,0:T(8,128)(2,1)}) %all-gather.11.cloned.1.call-update) | async-done | bytes 16777232 | tf_op jit(solution)/shard_map/all_gather | solution.py:81
  944.3 14.5 copy_bitcast_fusion.2
  958.8 6.4 gather_fusion.3
  965.2 1.7 fusion.28
  966.9 11.3 broadcast.314
  978.2 2.6 broadcast.315
  980.7 20.4 %while.91 = (s32[]{:T(128)}, f32[32,2048,128]{2,0,1:T(8,128)}, f32[32,256,128]{2,0,1:T(8,128)}, s32[]{:T(128)}, s32[64]{0:T(128)S(1)}, /*index=5*/s32[]{:T(128)}...) while((s32[]{:T(128)}, f32[32,2048,128]{2,0,1:T(8,128)}, ...), condition=%wide.region_18.21_spmd.clone, body=%wide.region_15.20_spmd.clone.sunk | while | flops 1049155 | bytes 10487937 | solution.py:69
  981.4 2.7 broadcast_multiply_fusion.9
  984.1 9.0 scatter_fusion.2
  993.1 8.0 scatter_fusion.3
  1001.1 4.4 copy_bitcast_fusion.4
  1005.6 22.6 %copy_bitcast_fusion = f32[32,262144]{1,0:T(8,128)} fusion(f32[32,2048,128]{2,0,1:T(8,128)} %get-tuple-element.613), kind=kLoop, calls=%fused_computation.68 | loop fusion | bytes 67108864 | tf_op jit(solution)/shard_map/reshape | solution.py:86
  1028.2 30.0 %reduce-scatter.11.cloned.1.call-done = f32[32,16384]{1,0:T(8,128)} async-done(((f32[32,32768]{1,0:T(8,128)}), f32[32,16384]{1,0:T(8,128)}) %reduce-scatter.11.cloned.1.call-update) | async-done | bytes 2097168 | tf_op jit(solution)/shard_map/reduce_scatter | solution.py:88
  1058.2 336.9 %reduce-scatter.9.cloned.1.call-done = f32[32,16384]{1,0:T(8,128)} async-done(((f32[32,262144]{1,0:T(8,128)}), f32[32,16384]{1,0:T(8,128)}) %reduce-scatter.9.cloned.1.call-update) | async-done | bytes 2097168 | tf_op jit(solution)/shard_map/reduce_scatter | solution.py:85
  1395.2 2.4 add.221
  1397.6 1.3 copy-done.1
  1398.9 1.8 fusion.53
  1400.7 39.0 %psum.15 = f32[32,32]{1,0:T(8,128)S(1)} all-reduce(f32[32,32]{1,0:T(8,128)S(1)} %fusion.53), channel_id=1, replica_groups=mesh['row'=2,'col'=16] {'row','col'}, use_global_device_ids=true, to_apply=%region_21.24 | all-reduce | flops 1024 | bytes 8192 | tf_op jit(solution)/shard_map/psum | solution.py:95
  1439.8 53.9 %while.94 = (s32[]{:T(128)}, f32[32,32]{1,0:T(8,128)S(1)}, f32[32,32]{0,1:T(8,128)S(1)}, s32[]{:T(128)}, s32[]{:T(128)}) while((s32[]{:T(128)}, f32[32,32]{1,0:T(8,128)S(1)}, f32[32,32]{0,1:T(8,128)S(1)}, s32[]{:T(128)}, s32[]{:T(128)}) %tuple.201), condition=%wide.region_25.28_spmd.clone.clone, body=%wide.region_22.27_spmd.clone.clone.sunk | while | flops 2401 | bytes 8913 | solution.py:26
  1493.7 44.3 %while.95 = (s32[]{:T(128)}, f32[32,32]{1,0:T(8,128)S(1)}, f32[32,32]{1,0:T(8,128)S(1)}, s32[]{:T(128)}, s32[]{:T(128)}) while((s32[]{:T(128)}, f32[32,32]{1,0:T(8,128)S(1)}, f32[32,32]{1,0:T(8,128)S(1)}, s32[]{:T(128)}, s32[]{:T(128)}) %tuple.204), condition=%wide.region_29.32_spmd.clone.clone, body=%wide.region_26.31_spmd.clone.clone.sunk | while | flops 2305 | bytes 6221 | solution.py:43
  1538.1 4.8 fusion.54
  (669 shorter events, 151.3 us)
Async XLA Ops:
  6.5 44.4 %copy-start = (bf16[64,128,128]{2,1,0:T(8,128)(2,1)S(1)}, bf16[64,128,128]{2,1,0:T(8,128)(2,1)}, u32[]{:S(2)}) copy-start(bf16[64,128,128]{2,1,0:T(8,128)(2,1)} %param.21) | copy-start | bytes 6291460
  6.5 4.3 copy-start.3
  6.5 4.4 copy-start.4
  6.5 38.8 %all-gather.5.cloned.1.call-start = ((), (), s32[]{:S(2)}) async-start(), calls=%async_computation.4 | async-start | bytes 3145728 | tf_op jit(solution)/shard_map/all_gather | solution.py:80
  9.4 165.1 %all-gather.7.cloned.1.call-start = ((), (), s32[]{:S(2)}) async-start(), calls=%async_computation.5 | async-start | bytes 17825792 | tf_op jit(solution)/shard_map/all_gather | solution.py:81
  10.2 278.3 %reduce-scatter.7.cloned.1.call-start = ((), (), s32[]{:S(2)}) async-start(), calls=%async_computation.7 | async-start | bytes 6291456 | tf_op jit(solution)/shard_map/reduce_scatter | solution.py:88
  235.8 390.0 %reduce-scatter.5.cloned.1.call-start = ((), (), s32[]{:S(2)}) async-start(), calls=%async_computation.6 | async-start | bytes 35651584 | tf_op jit(solution)/shard_map/reduce_scatter | solution.py:85
  258.4 556.7 %all-gather.9.cloned.1.call-start = ((), (), s32[]{:S(2)}) async-start(), calls=%async_computation.8 | async-start | bytes 3145728 | tf_op jit(solution)/shard_map/all_gather | solution.py:80
  628.2 1.3 copy-start.2
  782.0 162.3 %all-gather.11.cloned.1.call-start = ((), (), s32[]{:S(2)}) async-start(), calls=%async_computation.9 | async-start | bytes 17825792 | tf_op jit(solution)/shard_map/all_gather | solution.py:81
  782.6 275.6 %reduce-scatter.11.cloned.1.call-start = ((), (), s32[]{:S(2)}) async-start(), calls=%async_computation.11 | async-start | bytes 6291456 | tf_op jit(solution)/shard_map/reduce_scatter | solution.py:88
  1005.6 389.6 %reduce-scatter.9.cloned.1.call-start = ((), (), s32[]{:S(2)}) async-start(), calls=%async_computation.10 | async-start | bytes 35651584 | tf_op jit(solution)/shard_map/reduce_scatter | solution.py:85
  1397.6 1.4 copy-start.1
Sparse Core Ops, SparseCore 0:
  9.5 35.8 all-gather.4
  47.6 126.9 all-gather.6
  235.9 52.4 reduce-scatter.6
  293.1 332.6 reduce-scatter.4
  782.1 32.8 all-gather.8
  817.4 126.9 all-gather.10
  1005.7 52.4 reduce-scatter.10
  1062.5 332.6 reduce-scatter.8
where the time goes:
time: 1550 us
  waiting for transfers between devices  1050 us (68%)
  other arithmetic  189 us (12%)
  local copies, waits for them, and re-layouts  153 us (10%)
  blocking collectives  78.1 us (5%)
  loops' own time  48.3 us (3%)
  matrix products  20.5 us (1%)
    reduce_scatter x2, waiting for transfers between devices, per_device(): lax.psum_scatter(row_sums.reshape(vector_count, -1), 'col', scatter_dimen...  674 us
    all_gather x2, waiting for transfers between devices, per_device(): row_panel = lax.all_gather(rounded, 'col', axis=1, tiled=True)  243 us
    psum x2, blocking collectives, per_device(): gram_matrix = lax.psum(local_gram, ('row', 'col')) / N  78.1 us
    all_gather x2, waiting for transfers between devices, per_device(): col_panel = lax.all_gather(rounded, 'row', axis=1, tiled=True)  66.7 us
    reduce_scatter x2, waiting for transfers between devices, per_device(): lax.psum_scatter(col_sums.reshape(vector_count, -1), 'row', scatter_dimen...  60 us
    another operation x2, loops' own time, cholesky_lower(): lax.fori_loop(0, matrix_order, column_step, jnp.zeros_like(gram_matrix))  46.9 us
    reshape x2, local copies, waits for them, and re-layouts, per_device(): row_sums.reshape(vector_count, -1)  45.2 us
    reduce_sum x64, other arithmetic, column_step(): pivot_value = jnp.sqrt(jnp.sum(jnp.where(on_diagonal, residue, 0.0)))  42.8 us
  transfers between devices with their start and end apart: 8, of which 8 were waited for; matrix products, arithmetic and copies ran while one was open for 4% of the time, Pallas kernels for 0%

commit v1 on v0

--- a/solution.py
+++ b/solution.py
@@ -92,7 +92,7 @@
         local_gram = jnp.dot(
             product, product.T, precision=lax.Precision.HIGHEST, preferred_element_type=jnp.float32
         )
-        gram_matrix = lax.psum(local_gram, ("row", "col")) / N
+        gram_matrix = lax.psum(lax.psum(local_gram, "col"), "row") / N
         inverse = lower_inverse(cholesky_lower(gram_matrix))
         vectors = jnp.dot(
             inverse, product, precision=lax.Precision.HIGHEST, preferred_element_type=jnp.float32

time: 1550 us -> 1610 us (1.039)
  blocking collectives: 78.1 us -> 135 us
    psum x2 -> x4, blocking collectives: 78.1 us -> 135 us  [per_device(): gram_matrix = lax.psum(lax.psum(local_gram, 'col'), 'row') / N]
where the time goes in v1:
time: 1610 us; the launch traced here: 1600 us
  waiting for transfers between devices  1040 us (65%)
  other arithmetic  189 us (12%)
  local copies, waits for them, and re-layouts  153 us (10%)
  blocking collectives  135 us (8%)
  loops' own time  48.3 us (3%)
  matrix products  20.5 us (1%)
    reduce_scatter x2, waiting for transfers between devices, per_device(): lax.psum_scatter(row_sums.reshape(vector_count, -1), 'col', scatter_dimen...  674 us
    all_gather x2, waiting for transfers between devices, per_device(): row_panel = lax.all_gather(rounded, 'col', axis=1, tiled=True)  243 us
    psum x4, blocking collectives, per_device(): gram_matrix = lax.psum(lax.psum(local_gram, 'col'), 'row') / N  135 us
    all_gather x2, waiting for transfers between devices, per_device(): col_panel = lax.all_gather(rounded, 'row', axis=1, tiled=True)  63.2 us
    reduce_scatter x2, waiting for transfers between devices, per_device(): lax.psum_scatter(col_sums.reshape(vector_count, -1), 'row', scatter_dimen...  60 us
    another operation x2, loops' own time, cholesky_lower(): lax.fori_loop(0, matrix_order, column_step, jnp.zeros_like(gram_matrix))  46.9 us
    reshape x2, local copies, waits for them, and re-layouts, per_device(): row_sums.reshape(vector_count, -1)  45.2 us
    reduce_sum x64, other arithmetic, column_step(): pivot_value = jnp.sqrt(jnp.sum(jnp.where(on_diagonal, residue, 0.0)))  42.8 us
  transfers between devices with their start and end apart: 8, of which 8 were waited for; matrix products, arithmetic and copies ran while one was open for 4% of the time, Pallas kernels for 0%

profile of v1, /device:TPU:0, one launch (start us, length us, event | category | flops | bytes accessed | tf_op | source)
XLA Modules:
  0.0 1603.6 jit_solution(4482185751931948693)
XLA Ops:
  6.5 2.8 convert_element_type.66
  9.4 0.7 all-gather.7.cloned.1.call-update
  11.0 34.4 %all-gather.5.cloned.1.call-done = bf16[32,32768]{1,0:T(8,128)(2,1)} async-done(((bf16[32,16384]{1,0:T(8,128)(2,1)}), bf16[32,32768]{1,0:T(8,128)(2,1)}) %all-gather.5.cloned.1.call-update) | async-done | bytes 2097168 | tf_op jit(solution)/shard_map/all_gather | solution.py:80
  45.4 3.3 copy_bitcast_fusion.7
  48.6 2.2 gather_fusion
  50.9 2.2 fusion.34
  53.1 121.4 %all-gather.7.cloned.1.call-done = bf16[32,262144]{1,0:T(8,128)(2,1)} async-done(((bf16[32,16384]{1,0:T(8,128)(2,1)}), bf16[32,262144]{1,0:T(8,128)(2,1)}) %all-gather.7.cloned.1.call-update) | async-done | bytes 16777232 | tf_op jit(solution)/shard_map/all_gather | solution.py:81
  174.5 14.5 copy_bitcast_fusion.3
  189.0 6.4 gather_fusion.1
  195.4 1.7 fusion.32
  197.1 11.3 broadcast.314.clone
  208.4 2.6 broadcast.315.clone
  210.9 20.4 %while.90 = (s32[]{:T(128)}, f32[32,2048,128]{2,0,1:T(8,128)}, f32[32,256,128]{2,0,1:T(8,128)}, s32[]{:T(128)}, s32[64]{0:T(128)S(1)}, /*index=5*/s32[]{:T(128)}...) while((s32[]{:T(128)}, f32[32,2048,128]{2,0,1:T(8,128)}, ...), condition=%wide.region_3.6_spmd.clone, body=%wide.region_0.5_spmd.clone.sunk | while | flops 1049155 | bytes 10487937 | solution.py:69
  211.6 2.7 broadcast_multiply_fusion.8
  214.3 9.0 scatter_fusion
  223.3 8.0 scatter_fusion.1
  231.3 4.4 copy_bitcast_fusion.5
  235.8 22.6 %copy_bitcast_fusion.1 = f32[32,262144]{1,0:T(8,128)} fusion(f32[32,2048,128]{2,0,1:T(8,128)} %get-tuple-element.609), kind=kLoop, calls=%fused_computation.69 | loop fusion | bytes 67108864 | tf_op jit(solution)/shard_map/reshape | solution.py:86
  258.5 30.0 %reduce-scatter.7.cloned.1.call-done = f32[32,16384]{1,0:T(8,128)} async-done(((f32[32,32768]{1,0:T(8,128)}), f32[32,16384]{1,0:T(8,128)}) %reduce-scatter.7.cloned.1.call-update) | async-done | bytes 2097168 | tf_op jit(solution)/shard_map/reduce_scatter | solution.py:88
  288.4 337.4 %reduce-scatter.5.cloned.1.call-done = f32[32,16384]{1,0:T(8,128)} async-done(((f32[32,262144]{1,0:T(8,128)}), f32[32,16384]{1,0:T(8,128)}) %reduce-scatter.5.cloned.1.call-update) | async-done | bytes 2097168 | tf_op jit(solution)/shard_map/reduce_scatter | solution.py:85
  625.8 2.4 add.224
  628.2 1.3 copy-done.2
  629.5 1.8 fusion.52
  631.3 59.6 %psum.28 = f32[32,32]{1,0:T(8,128)S(1)} all-reduce(f32[32,32]{1,0:T(8,128)S(1)} %fusion.52), channel_id=1, replica_groups=mesh['row'=2,'col'=16] {'col'}, use_global_device_ids=true, to_apply=%region_6.9 | all-reduce | flops 1024 | bytes 8192 | tf_op jit(solution)/shard_map/psum | solution.py:95
  690.9 8.1 psum.29
  699.1 58.1 %while.92 = (s32[]{:T(128)}, f32[32,32]{1,0:T(8,128)S(1)}, f32[32,32]{0,1:T(8,128)S(1)}, s32[]{:T(128)}, s32[]{:T(128)}) while((s32[]{:T(128)}, f32[32,32]{1,0:T(8,128)S(1)}, f32[32,32]{0,1:T(8,128)S(1)}, s32[]{:T(128)}, s32[]{:T(128)}) %tuple.192), condition=%wide.region_11.14_spmd.clone.clone, body=%wide.region_8.13_spmd.clone.clone.sunk | while | flops 2401 | bytes 8913 | solution.py:26
  699.3 0.7 fusion.88
  701.0 0.7 fusion.88
  702.8 0.7 fusion.88
  704.6 0.7 fusion.88
  710.1 0.7 fusion.88
  715.6 0.7 fusion.88
  733.8 0.7 fusion.88
  739.2 0.7 fusion.88
  744.7 0.7 fusion.88
  750.1 0.7 fusion.88
  757.3 49.0 %while.93 = (s32[]{:T(128)}, f32[32,32]{1,0:T(8,128)S(1)}, f32[32,32]{1,0:T(8,128)S(1)}, s32[]{:T(128)}, s32[]{:T(128)}) while((s32[]{:T(128)}, f32[32,32]{1,0:T(8,128)S(1)}, f32[32,32]{1,0:T(8,128)S(1)}, s32[]{:T(128)}, s32[]{:T(128)}) %tuple.195), condition=%wide.region_15.18_spmd.clone.clone, body=%wide.region_12.17_spmd.clone.clone.sunk | while | flops 2305 | bytes 6221 | solution.py:43
  806.2 4.4 convolution_convert_fusion
  811.5 28.8 %all-gather.9.cloned.1.call-done = bf16[32,32768]{1,0:T(8,128)(2,1)} async-done(((bf16[32,16384]{1,0:T(8,128)(2,1)}), bf16[32,32768]{1,0:T(8,128)(2,1)}) %all-gather.9.cloned.1.call-update) | async-done | bytes 2097168 | tf_op jit(solution)/shard_map/all_gather | solution.py:80
  840.3 3.3 copy_bitcast_fusion.6
  843.6 2.2 gather_fusion.2
  845.8 2.2 fusion.30
  848.0 121.5 %all-gather.11.cloned.1.call-done = bf16[32,262144]{1,0:T(8,128)(2,1)} async-done(((bf16[32,16384]{1,0:T(8,128)(2,1)}), bf16[32,262144]{1,0:T(8,128)(2,1)}) %all-gather.11.cloned.1.call-update) | async-done | bytes 16777232 | tf_op jit(solution)/shard_map/all_gather | solution.py:81
  969.5 14.5 copy_bitcast_fusion.2
  984.0 6.4 gather_fusion.3
  990.5 1.7 fusion.28
  992.1 11.3 broadcast.314
  1003.4 2.6 broadcast.315
  1006.0 20.4 %while.91 = (s32[]{:T(128)}, f32[32,2048,128]{2,0,1:T(8,128)}, f32[32,256,128]{2,0,1:T(8,128)}, s32[]{:T(128)}, s32[64]{0:T(128)S(1)}, /*index=5*/s32[]{:T(128)}...) while((s32[]{:T(128)}, f32[32,2048,128]{2,0,1:T(8,128)}, ...), condition=%wide.region_19.22_spmd.clone, body=%wide.region_16.21_spmd.clone.sunk | while | flops 1049155 | bytes 10487937 | solution.py:69
  1006.6 2.7 broadcast_multiply_fusion.9
  1009.3 9.0 scatter_fusion.2
  1018.3 8.0 scatter_fusion.3
  1026.3 4.4 copy_bitcast_fusion.4
  1030.8 22.6 %copy_bitcast_fusion = f32[32,262144]{1,0:T(8,128)} fusion(f32[32,2048,128]{2,0,1:T(8,128)} %get-tuple-element.613), kind=kLoop, calls=%fused_computation.68 | loop fusion | bytes 67108864 | tf_op jit(solution)/shard_map/reshape | solution.py:86
  1053.4 30.0 %reduce-scatter.11.cloned.1.call-done = f32[32,16384]{1,0:T(8,128)} async-done(((f32[32,32768]{1,0:T(8,128)}), f32[32,16384]{1,0:T(8,128)}) %reduce-scatter.11.cloned.1.call-update) | async-done | bytes 2097168 | tf_op jit(solution)/shard_map/reduce_scatter | solution.py:88
  1083.4 336.9 %reduce-scatter.9.cloned.1.call-done = f32[32,16384]{1,0:T(8,128)} async-done(((f32[32,262144]{1,0:T(8,128)}), f32[32,16384]{1,0:T(8,128)}) %reduce-scatter.9.cloned.1.call-update) | async-done | bytes 2097168 | tf_op jit(solution)/shard_map/reduce_scatter | solution.py:85
  1420.4 2.4 add.225
  1422.8 1.3 copy-done.1
  1424.2 1.8 fusion.53
  1425.9 59.6 %psum.30 = f32[32,32]{1,0:T(8,128)S(1)} all-reduce(f32[32,32]{1,0:T(8,128)S(1)} %fusion.53), channel_id=1, replica_groups=mesh['row'=2,'col'=16] {'col'}, use_global_device_ids=true, to_apply=%region_22.25 | all-reduce | flops 1024 | bytes 8192 | tf_op jit(solution)/shard_map/psum | solution.py:95
  1485.5 8.1 psum.31
  1493.7 53.9 %while.94 = (s32[]{:T(128)}, f32[32,32]{1,0:T(8,128)S(1)}, f32[32,32]{0,1:T(8,128)S(1)}, s32[]{:T(128)}, s32[]{:T(128)}) while((s32[]{:T(128)}, f32[32,32]{1,0:T(8,128)S(1)}, f32[32,32]{0,1:T(8,128)S(1)}, s32[]{:T(128)}, s32[]{:T(128)}) %tuple.201), condition=%wide.region_27.30_spmd.clone.clone, body=%wide.region_24.29_spmd.clone.clone.sunk | while | flops 2401 | bytes 8913 | solution.py:26
  1547.7 44.3 %while.95 = (s32[]{:T(128)}, f32[32,32]{1,0:T(8,128)S(1)}, f32[32,32]{1,0:T(8,128)S(1)}, s32[]{:T(128)}, s32[]{:T(128)}) while((s32[]{:T(128)}, f32[32,32]{1,0:T(8,128)S(1)}, f32[32,32]{1,0:T(8,128)S(1)}, s32[]{:T(128)}, s32[]{:T(128)}) %tuple.204), condition=%wide.region_31.34_spmd.clone.clone, body=%wide.region_28.33_spmd.clone.clone.sunk | while | flops 2305 | bytes 6221 | solution.py:43
  1592.0 4.8 fusion.54
  (671 shorter events, 152.7 us)
Async XLA Ops:
  6.5 44.4 %copy-start = (bf16[64,128,128]{2,1,0:T(8,128)(2,1)S(1)}, bf16[64,128,128]{2,1,0:T(8,128)(2,1)}, u32[]{:S(2)}) copy-start(bf16[64,128,128]{2,1,0:T(8,128)(2,1)} %param.21) | copy-start | bytes 6291460
  6.5 4.3 copy-start.3
  6.5 4.4 copy-start.4
  6.5 38.8 %all-gather.5.cloned.1.call-start = ((), (), s32[]{:S(2)}) async-start(), calls=%async_computation.4 | async-start | bytes 3145728 | tf_op jit(solution)/shard_map/all_gather | solution.py:80
  9.4 165.1 %all-gather.7.cloned.1.call-start = ((), (), s32[]{:S(2)}) async-start(), calls=%async_computation.5 | async-start | bytes 17825792 | tf_op jit(solution)/shard_map/all_gather | solution.py:81
  10.2 278.3 %reduce-scatter.7.cloned.1.call-start = ((), (), s32[]{:S(2)}) async-start(), calls=%async_computation.7 | async-start | bytes 6291456 | tf_op jit(solution)/shard_map/reduce_scatter | solution.py:88
  235.8 390.0 %reduce-scatter.5.cloned.1.call-start = ((), (), s32[]{:S(2)}) async-start(), calls=%async_computation.6 | async-start | bytes 35651584 | tf_op jit(solution)/shard_map/reduce_scatter | solution.py:85
  258.4 581.9 %all-gather.9.cloned.1.call-start = ((), (), s32[]{:S(2)}) async-start(), calls=%async_computation.8 | async-start | bytes 3145728 | tf_op jit(solution)/shard_map/all_gather | solution.py:80
  628.2 1.3 copy-start.2
  810.7 158.8 %all-gather.11.cloned.1.call-start = ((), (), s32[]{:S(2)}) async-start(), calls=%async_computation.9 | async-start | bytes 17825792 | tf_op jit(solution)/shard_map/all_gather | solution.py:81
  811.3 272.2 %reduce-scatter.11.cloned.1.call-start = ((), (), s32[]{:S(2)}) async-start(), calls=%async_computation.11 | async-start | bytes 6291456 | tf_op jit(solution)/shard_map/reduce_scatter | solution.py:88
  1030.8 389.6 %reduce-scatter.9.cloned.1.call-start = ((), (), s32[]{:S(2)}) async-start(), calls=%async_computation.10 | async-start | bytes 35651584 | tf_op jit(solution)/shard_map/reduce_scatter | solution.py:85
  1422.8 1.4 copy-start.1
Sparse Core Ops, SparseCore 0:
  9.5 35.8 all-gather.4
  47.6 126.9 all-gather.6
  235.9 52.4 reduce-scatter.6
  293.1 332.6 reduce-scatter.4
  810.8 29.4 all-gather.8
  842.6 126.9 all-gather.10
  1030.9 52.4 reduce-scatter.10
  1087.7 332.6 reduce-scatter.8
